TPU v7x, 32 devices: a whole 2x2x4 slice. The times are simulated.
32 devices in a mesh: groups: 2 (over x), mem: 8 (over z, y), tp: 2 (over core).
Axes of the slice: x: 2, y: 2, z: 4, core: 2. Of those that a mesh axis runs over, the one named last changes fastest.
Arguments:
- hidden: bfloat16 [128, 8192], P('groups', 'mem'), parts along dimension 0, may hold values from -6 to 6
- adapter: int32 [128], P('groups'), parts along dimension 0, may hold values from 0 to 31
- page_cache_slot: int32 [256], P('groups'), parts along dimension 0, may hold values from 0 to 127, as said below
- selection: int32 [128, 128], P('groups'), parts along dimension 0, may hold values from 0 to 1, as said below
- query_projection_weight: bfloat16 [8192, 8192], P('mem', 'tp'), may hold values from -0.0625 to 0.0625
- key_projection_weight: bfloat16 [8192, 1024], P('mem', 'tp'), may hold values from -0.0625 to 0.0625
- value_projection_weight: bfloat16 [8192, 1024], P('mem', 'tp'), may hold values from -0.0625 to 0.0625
- adapter_down_weight: bfloat16 [8192, 2048], P('mem'), may hold values from -0.0625 to 0.0625
- adapter_up_weight: bfloat16 [64, 32, 8192], P('mem', None, 'tp'), may hold values from -0.75 to 0.75
- output_projection_weight: bfloat16 [8192, 8192], P('tp', 'mem'), may hold values from -0.0625 to 0.0625
- prefix_key_cache: bfloat16 [256, 128, 1024], P(('groups', 'mem'), None, 'tp'), parts along dimension 0, may hold values from -60 to 60
- prefix_value_cache: bfloat16 [256, 128, 1024], P(('groups', 'mem'), None, 'tp'), parts along dimension 0, may hold values from -6 to 6
Outputs:
- attn_out: bfloat16 [128, 8192], P('groups', 'mem'), parts along dimension 0
There are 2 independent parts, one for each index of `groups`. A program takes and returns all parts, laid end to end along the dimension named above; an argument that names none is the same for every part. Nothing has to cross between parts.
Inputs may be any that keep to these rules, and one draw needn't show every extreme that they name: A permutation: page p is held in cache slot page_cache_slot[p], and slot s lies with index s // 16 of mem. `selection`: every page is selected by 1 to 32 forks; on some index of mem every page held there is selected by exactly 32 forks. A fork may select no page.
All inputs are finite; a program needn't handle non-finite values.
Results may differ from a plain program's by a relative error of at most 0.006.
The roundings to bfloat16 on the way count: a program that leaves them out, or rounds other values in their place, can miss the bound.
Values may be sent and summed in bfloat16 or wider, within the bound.
A program may use at most 128 MiB of HBM per device.

v0:
```python
import jax
import jax.numpy as jnp
from jax import lax
from jax.sharding import PartitionSpec as P

HEAD_WIDTH = 128
ADAPTER_RANK = 64
ADAPTER_COUNT = 32
HOT = 32


adapter_scale = 1.0
neg_floor = -1e30


def shards(
    hidden,
    adapter,
    page_cache_slot,
    selection,
    query_projection_weight,
    key_projection_weight,
    value_projection_weight,
    adapter_down_weight,
    adapter_up_weight,
    output_projection_weight,
    prefix_key_cache,
    prefix_value_cache,
):
    mem_count = lax.axis_size("mem")
    mem_index = lax.axis_index("mem")
    every_fork_list = hidden.shape[0]
    fork_own = every_fork_list // mem_count
    query_total_width = query_projection_weight.shape[1]
    kv_local = key_projection_weight.shape[1] // HEAD_WIDTH
    heads_local = query_total_width // HEAD_WIDTH
    group_size = heads_local // kv_local
    page_local = prefix_key_cache.shape[0]
    page_len = prefix_key_cache.shape[1]
    score_scale = HEAD_WIDTH ** (-0.5)
    onehot = (adapter[:, None] == jnp.arange(ADAPTER_COUNT, dtype=jnp.int32)[None, :]).astype(
        jnp.float32
    )
    down_activations = jnp.dot(
        hidden, adapter_down_weight, preferred_element_type=jnp.float32
    ).reshape(every_fork_list, ADAPTER_COUNT, ADAPTER_RANK)
    rank_part = jnp.sum(down_activations * onehot[:, :, None], axis=1)
    rank_acts = lax.psum_scatter(rank_part, "mem", scatter_dimension=1, tiled=True).astype(
        jnp.bfloat16
    )
    rank_slice_local = rank_acts.shape[1]
    spread_factor = (rank_acts.astype(jnp.float32)[:, :, None] * onehot[:, None, :]).astype(
        jnp.bfloat16
    )
    spread_factor = spread_factor.reshape(every_fork_list, rank_slice_local * ADAPTER_COUNT)
    adapter_query_delta = jnp.dot(
        spread_factor,
        adapter_up_weight.reshape(rank_slice_local * ADAPTER_COUNT, query_total_width),
        preferred_element_type=jnp.float32,
    )
    query_part = (
        jnp.dot(hidden, query_projection_weight, preferred_element_type=jnp.float32)
        + adapter_scale * adapter_query_delta
    )
    key_part = jnp.dot(hidden, key_projection_weight, preferred_element_type=jnp.float32)
    value_part = jnp.dot(hidden, value_projection_weight, preferred_element_type=jnp.float32)
    query_sum, key_sum, value_sum = lax.psum((query_part, key_part, value_part), "mem")
    query_all = query_sum.astype(jnp.bfloat16)
    query_own = lax.dynamic_slice_in_dim(query_all, mem_index * fork_own, fork_own, 0)
    key_own = lax.dynamic_slice_in_dim(key_sum, mem_index * fork_own, fork_own, 0).astype(
        jnp.bfloat16
    )
    value_own = lax.dynamic_slice_in_dim(value_sum, mem_index * fork_own, fork_own, 0).astype(
        jnp.bfloat16
    )
    page_total = page_cache_slot.shape[0]
    slot_ids = mem_index * page_local + jnp.arange(page_local, dtype=jnp.int32)
    slot_match = page_cache_slot[None, :] == slot_ids[:, None]
    page_of = jnp.sum(
        jnp.where(slot_match, jnp.arange(page_total, dtype=jnp.int32)[None, :], 0), axis=1
    )
    columns = jnp.take(selection, page_of, axis=1).T
    ranking = jnp.cumsum(columns, axis=1) - 1
    slot_hits = (columns[:, :, None] > 0) & (
        ranking[:, :, None] == jnp.arange(HOT, dtype=jnp.int32)[None, None, :]
    )
    fork_ids = jnp.arange(every_fork_list, dtype=jnp.int32)[None, :, None]
    fork_of = jnp.sum(jnp.where(slot_hits, fork_ids, 0), axis=1) + jnp.where(
        jnp.any(slot_hits, axis=1), 0, every_fork_list
    )
    query_pad = jnp.concatenate(
        [query_all, jnp.zeros((1, query_total_width), jnp.bfloat16)], axis=0
    )
    picked = query_pad[fork_of].reshape(page_local, HOT, kv_local, group_size, HEAD_WIDTH)
    page_keys = prefix_key_cache.reshape(page_local, page_len, kv_local, HEAD_WIDTH)
    page_values = prefix_value_cache.reshape(page_local, page_len, kv_local, HEAD_WIDTH)
    scores = (
        jnp.einsum("phkgd,ptkd->phkgt", picked, page_keys, preferred_element_type=jnp.float32)
        * score_scale
    )
    page_peak = jnp.max(scores, axis=-1)
    weights = jnp.exp(scores - page_peak[..., None]).astype(jnp.bfloat16)
    masses = jnp.sum(weights.astype(jnp.float32), axis=-1)
    partial_value = jnp.einsum(
        "phkgt,ptkd->phkgd", weights, page_values, preferred_element_type=jnp.float32
    )
    pair_count = page_local * HOT
    owners = fork_of.reshape(pair_count)
    peak_flat = page_peak.reshape(pair_count, heads_local)
    pair_hit = owners[None, :] == jnp.arange(every_fork_list + 1, dtype=jnp.int32)[:, None]
    pair_float = pair_hit.astype(jnp.float32)
    maxima_all = jnp.max(jnp.where(pair_hit[:, :, None], peak_flat[None, :, :], neg_floor), axis=1)
    owner_max = jnp.dot(pair_float.T, maxima_all, precision=lax.Precision.HIGHEST)
    rescale = jnp.exp(peak_flat - owner_max)
    mass_scaled = masses.reshape(pair_count, heads_local) * rescale
    acc_scaled = (
        partial_value.reshape(pair_count, heads_local, HEAD_WIDTH) * rescale[:, :, None]
    ).reshape(pair_count, query_total_width)
    totals = jnp.dot(pair_float, mass_scaled, precision=lax.Precision.HIGHEST)[:every_fork_list]
    summed = jnp.dot(pair_float, acc_scaled, precision=lax.Precision.HIGHEST)[
        :every_fork_list
    ].reshape(every_fork_list, heads_local, HEAD_WIDTH)
    maxima = maxima_all[:every_fork_list]
    summed_flat = summed.reshape(every_fork_list, query_total_width)
    max_in, total_in, sum_in = (
        lax.all_to_all(maxima, "mem", split_axis=0, concat_axis=0, tiled=True),
        lax.all_to_all(totals, "mem", split_axis=0, concat_axis=0, tiled=True),
        lax.all_to_all(summed_flat, "mem", split_axis=0, concat_axis=0, tiled=True),
    )
    max_in = max_in.reshape(mem_count, fork_own, heads_local)
    total_in = total_in.reshape(mem_count, fork_own, heads_local)
    sum_in = sum_in.reshape(mem_count, fork_own, heads_local, HEAD_WIDTH)
    cache_max = jnp.max(max_in, axis=0)
    factor = jnp.exp(max_in - cache_max[None])
    cache_total = jnp.sum(total_in * factor, axis=0)
    cache_sum = jnp.sum(sum_in * factor[..., None], axis=0)
    query_f = query_own.reshape(fork_own, kv_local, group_size, HEAD_WIDTH).astype(jnp.float32)
    key_f = key_own.reshape(fork_own, kv_local, 1, HEAD_WIDTH).astype(jnp.float32)
    own_score = (jnp.sum(query_f * key_f, axis=-1) * score_scale).reshape(fork_own, heads_local)
    value_f = jnp.broadcast_to(
        value_own.reshape(fork_own, kv_local, 1, HEAD_WIDTH).astype(jnp.float32),
        (fork_own, kv_local, group_size, HEAD_WIDTH),
    ).reshape(fork_own, heads_local, HEAD_WIDTH)
    final_max = jnp.maximum(cache_max, own_score)
    old_weight = jnp.exp(cache_max - final_max)
    own_weight = jnp.exp(own_score - final_max)
    normalized = (cache_sum * old_weight[..., None] + own_weight[..., None] * value_f) / (
        cache_total * old_weight + own_weight
    )[..., None]
    attended = normalized.astype(jnp.bfloat16).reshape(fork_own, query_total_width)
    projected = jnp.dot(
        lax.all_gather(attended, "mem", axis=0, tiled=True),
        output_projection_weight,
        preferred_element_type=jnp.float32,
    )
    return lax.psum(projected, "tp").astype(jnp.bfloat16)


def solution(mesh):
    return jax.shard_map(
        shards,
        mesh=mesh,
        in_specs=(
            P("groups", "mem"),
            P("groups"),
            P("groups"),
            P("groups", None),
            P("mem", "tp"),
            P("mem", "tp"),
            P("mem", "tp"),
            P("mem", None),
            P("mem", None, "tp"),
            P("tp", "mem"),
            P(("groups", "mem"), None, "tp"),
            P(("groups", "mem"), None, "tp"),
        ),
        out_specs=P("groups", "mem"),
        check_vma=False,
    )
```

profile of v0, /device:TPU:0, one launch (start us, length us, event | category | flops | bytes accessed | tf_op | source)
XLA Modules:
  0.0 277.6 jit_solution(2105505733350304345)
XLA Ops:
  4.5 1.6 fusion.35
  6.1 2.3 fusion.36
  8.4 3.9 %fusion.34 = f32[64,2048]{1,0:T(8,128)} fusion(bf16[64,1024]{1,0:T(8,128)(2,1)} %param.12, bf16[1024,2048]{1,0:T(8,128)(2,1)} %param.19), kind=kOutput, calls=%fused_computation.77 | convolution fusion | flops 268435456 | bytes 4849664 | tf_op jit(solution)/shard_map/dot_general | solution.py:44
  14.2 38.9 %all-reduce.1 = bf16[64,64]{0,1:T(8,128)(2,1)S(1)} all-reduce(f32[64,64]{0,1:T(8,128)S(1)} %copy.68), channel_id=2, replica_groups=mesh['groups'=2,'mem'=8,'tp'=2] {'mem'}, use_global_device_ids=true, to_apply=%region_5.6.clone | all-reduce | flops 4096 | bytes 24576
  55.0 5.0 %convolution_add_fusion = f32[64,4096]{1,0:T(8,128)S(1)} fusion(f32[64,4096]{1,0:T(8,128)S(1)} %convolution_bitcast_fusion, bf16[64,1024]{1,0:T(8,128)(2,1)S(1)} %copy-done.6, bf16[1024,4096]{1,0:T(8,128)(2,1)} %param.16), kind=kOutput, calls=%fused_computation.11 | convolution fusion | flops 537133056 | bytes 10616832 | tf_op jit(solution)/shard_map/dot_general | solution.py:62
  60.0 4.0 %reshape.245 = bf16[16,128,4,128]{3,2,1,0:T(4,128)(2,1)} reshape(bf16[16,128,512]{2,1,0:T(8,128)(2,1)} %param.22) | data formatting | bytes 4194304 | tf_op jit(solution)/shard_map/reshape | solution.py:95
  64.0 74.8 %all-reduce.5 = (bf16[64,512]{1,0:T(8,128)(2,1)S(1)}, bf16[64,4096]{1,0:T(8,128)(2,1)S(1)}, bf16[64,512]{1,0:T(8,128)(2,1)S(1)}) all-reduce(f32[64,512]{1,0:T(8,128)S(1)} %copy-done.7, f32[64,4096]{1,0:T(8,128)S(1)} %convolution_add_fusion, f32[64,512]{1,0:T(8,128)S(1)} %fusion.35), channel_id=1, replica_groups=mesh['groups'=2,'mem'=8,'tp'=2] {'mem'}, use_global_device_ids=true, to_apply=%region_13.14 | all-reduce | flops 327680 | bytes 1966080 | tf_op jit(solution)/shard_map/psum | solution.py:67
  138.8 4.4 %gather_fusion.1 = bf16[512,4096]{1,0:T(8,128)(2,1)} fusion(bf16[65,4096]{1,0:T(8,128)(2,1)S(1)} %concatenate.3, s32[1024]{0:T(1024)S(1)} %pad_clamp_fusion), kind=kCustom, calls=%fused_computation.1 | custom fusion | bytes 8390656 | tf_op jit(solution)/shard_map/gather | solution.py:94
  143.2 3.6 %copy.90 = bf16[64,8,32,128]{3,2,1,0:T(8,128)(2,1)S(1)} copy(bf16[64,8,32,128]{3,1,2,0:T(8,128)(2,1)} %bitcast.96) | data formatting | bytes 8388608
  146.8 5.7 %bitcast_reduce_fusion = (f32[16,32,4,8]{3,1,2,0:T(8,128)S(1)}, f32[16,4,32,8,128]{4,3,2,1,0:T(8,128)}) fusion(bf16[16,128,4,128,1]{3,2,1,0,4:T(4,128)(2,1)S(1)} %bitcast.98, bf16[16,32,4,8,128]{4,3,2,1,0:T(8,128)(2,1)S(1)} %bitcast.97), kind=kOutput, calls=%fused_computation.6 | convolution fusion | flops 541048832 | bytes 14745600 | tf_op jit(solution)/shard_map/phkgd,ptkd->phkgt/dot_general | solution.py:98
  154.1 3.5 %all-to-all-start.1 = ((f32[8,1,256]{2,1,0:T(1,128)}), f32[8,1,256]{2,1,0:T(1,128)S(1)}, u32[]{:S(2)}, u32[]{:S(2)}) async-start(f32[8,1,256]{2,1,0:T(1,128)} %reshape.276), calls=%async_computation.1 | async-start | bytes 16384 | tf_op jit(solution)/shard_map/all_to_all | solution.py:126
  157.8 4.0 %reshape.246 = bf16[16,128,4,128]{3,2,1,0:T(4,128)(2,1)} reshape(bf16[16,128,512]{2,1,0:T(8,128)(2,1)} %param.23) | data formatting | bytes 4194304 | tf_op jit(solution)/shard_map/reshape | solution.py:96
  161.9 8.2 %convert_reduce_fusion = f32[16,32,4,8]{3,1,2,0:T(8,128)S(1)} fusion(f32[16,32,4,8]{3,1,2,0:T(8,128)S(1)} %get-tuple-element.17, f32[16,4,32,8,128]{4,3,2,1,0:T(8,128)} %get-tuple-element.18), kind=kLoop, calls=%fused_computation.9 | loop fusion | flops 10469376 | bytes 8519680 | tf_op jit(solution)/shard_map/reduce_sum | solution.py:103
  170.1 4.9 %convolution_bitcast_fusion.1 = f32[16,32,4,8,128]{4,3,1,2,0:T(8,128)} fusion(bf16[16,128,4,128,1]{3,2,1,0,4:T(4,128)(2,1)S(1)} %bitcast.99, f32[16,4,32,8,128]{4,3,2,1,0:T(8,128)S(1)} %copy-done.2, f32[16,32,4,8]{3,1,2,0:T(8,128)S(1)} %get-tuple-element.17), kind=kOutput, calls=%fused_computation.16 | convolution fusion | flops 543162368 | bytes 18939904 | tf_op jit(solution)/shard_map/phkgt,ptkd->phkgd/dot_general | solution.py:104
  176.5 7.7 %copy.73 = f32[16,32,4,8,128]{4,3,2,1,0:T(8,128)} copy(f32[16,32,4,8,128]{4,3,1,2,0:T(8,128)} %convolution_bitcast_fusion.1) | data formatting | bytes 16777216 | tf_op jit(solution)/shard_map/phkgt,ptkd->phkgd/transpose | solution.py:104
  184.3 9.4 %reshape.247 = f32[512,4096]{1,0:T(8,128)} reshape(f32[16,32,4,8,128]{4,3,2,1,0:T(8,128)} %copy.73) | data formatting | bytes 16777216 | tf_op jit(solution)/shard_map/reshape | solution.py:117
  193.7 6.0 %all-to-all-start.2 = ((f32[8,1,256]{2,1,0:T(1,128)}), f32[8,1,256]{2,1,0:T(1,128)S(1)}, u32[]{:S(2)}, u32[]{:S(2)}) async-start(f32[8,1,256]{2,1,0:T(1,128)} %reshape.278), calls=%async_computation.2 | async-start | bytes 16384 | tf_op jit(solution)/shard_map/all_to_all | solution.py:127
  199.6 2.3 mul.132
  203.0 9.2 %fusion.4 = f32[8,8,4096]{2,1,0:T(8,128)} fusion(f32[512,4096]{1,0:T(8,128)S(1)} %copy-done.3, f32[64,8,32,128]{3,2,1,0:T(8,128)S(1)} %bitcast.95, pred[65,512]{1,0:T(8,128)(4,1)S(1)} %iota_compare_fusion.1), kind=kOutput, calls=%fused_computation.10 | convolution fusion | flops 1612709888 | bytes 17858560 | tf_op jit(solution)/shard_map/dot_general | solution.py:120
  212.2 6.0 %all-to-all-start = ((f32[8,8,4096]{2,1,0:T(8,128)}), f32[8,8,4096]{2,1,0:T(8,128)S(1)}, u32[]{:S(2)}, u32[]{:S(2)}) async-start(f32[8,8,4096]{2,1,0:T(8,128)} %fusion.4), calls=%async_computation | async-start | bytes 2097152 | tf_op jit(solution)/shard_map/all_to_all | solution.py:128
  220.8 15.3 %all-to-all-done = f32[8,8,4096]{2,1,0:T(8,128)S(1)} async-done(((f32[8,8,4096]{2,1,0:T(8,128)}), f32[8,8,4096]{2,1,0:T(8,128)S(1)}, u32[]{:S(2)}, u32[]{:S(2)}) %all-to-all-start) | async-done | bytes 1048608 | tf_op jit(solution)/shard_map/all_to_all | solution.py:128
  236.6 31.3 %all_gather.3 = bf16[64,4096]{1,0:T(8,128)(2,1)S(1)} all-gather(bf16[8,4096]{1,0:T(8,128)(2,1)S(1)} %fusion.14), channel_id=1, replica_groups=mesh['groups'=2,'mem'=8,'tp'=2] {'mem'}, dimensions={0}, use_global_device_ids=true | all-gather | bytes 589824 | tf_op jit(solution)/shard_map/all_gather | solution.py:152
  267.9 5.0 %fusion.37 = f32[64,1024]{1,0:T(8,128)S(1)} fusion(bf16[64,4096]{1,0:T(8,128)(2,1)S(1)} %all_gather.3, bf16[4096,1024]{1,0:T(8,128)(2,1)} %param.21), kind=kOutput, calls=%fused_computation.80 | convolution fusion | flops 536870912 | bytes 9175040 | tf_op jit(solution)/shard_map/dot_general | solution.py:151
  272.9 4.7 %all-reduce.6 = bf16[64,1024]{1,0:T(8,128)(2,1)} all-reduce(f32[64,1024]{1,0:T(8,128)S(1)} %fusion.37), channel_id=1, replica_groups=mesh['groups'=2,'mem'=8,'tp'=2] {'tp'}, use_global_device_ids=true, to_apply=%region_16.17 | all-reduce | flops 65536 | bytes 393216 | tf_op jit(solution)/shard_map/psum | solution.py:156
  (77 shorter events, 15.1 us)
Async XLA Ops:
  0.0 54.5 %copy-start = (bf16[8,32,4096]{2,1,0:T(8,128)(2,1)S(1)}, bf16[8,32,4096]{2,1,0:T(8,128)(2,1)}, u32[]{:S(2)}) copy-start(bf16[8,32,4096]{2,1,0:T(8,128)(2,1)} %param.20) | copy-start | bytes 6291460
  0.0 53.1 %copy-start.8 = (u32[32]{0:T(128)S(1)}, u32[32]{0:T(128)}, u32[]{:S(2)}) copy-start(u32[32]{0:T(128)} %constant.56) | copy-start | bytes 388
  0.0 55.0 %copy-start.6 = (bf16[64,1024]{1,0:T(8,128)(2,1)S(1)}, bf16[64,1024]{1,0:T(8,128)(2,1)}, u32[]{:S(2)}) copy-start(bf16[64,1024]{1,0:T(8,128)(2,1)} %param.12) | copy-start | bytes 393220
  55.0 9.0 %copy-start.7 = (f32[64,512]{1,0:T(8,128)S(1)}, f32[64,512]{1,0:T(8,128)}, u32[]{:S(2)}) copy-start(f32[64,512]{1,0:T(8,128)} %fusion.36) | copy-start | bytes 393220
  143.2 3.6 %copy-start.4 = (bf16[16,128,4,128]{3,2,1,0:T(4,128)(2,1)S(1)}, bf16[16,128,4,128]{3,2,1,0:T(4,128)(2,1)}, u32[]{:S(2)}) copy-start(bf16[16,128,4,128]{3,2,1,0:T(4,128)(2,1)} %reshape.245) | copy-start | bytes 6291460
  154.1 39.6 %all-to-all-start.1 = ((f32[8,1,256]{2,1,0:T(1,128)}), f32[8,1,256]{2,1,0:T(1,128)S(1)}, u32[]{:S(2)}, u32[]{:S(2)}) async-start(f32[8,1,256]{2,1,0:T(1,128)} %reshape.276), calls=%async_computation.1 | async-start | bytes 16384 | tf_op jit(solution)/shard_map/all_to_all | solution.py:126
  161.9 8.2 %copy-start.2 = (f32[16,4,32,8,128]{4,3,2,1,0:T(8,128)S(1)}, f32[16,4,32,8,128]{4,3,2,1,0:T(8,128)}, u32[]{:S(2)}) copy-start(f32[16,4,32,8,128]{4,3,2,1,0:T(8,128)} %get-tuple-element.18) | copy-start | bytes 25165828
  161.9 8.2 %copy-start.5 = (bf16[16,128,4,128]{3,2,1,0:T(4,128)(2,1)S(1)}, bf16[16,128,4,128]{3,2,1,0:T(4,128)(2,1)}, u32[]{:S(2)}) copy-start(bf16[16,128,4,128]{3,2,1,0:T(4,128)(2,1)} %reshape.246) | copy-start | bytes 6291460
  193.7 18.5 %all-to-all-start.2 = ((f32[8,1,256]{2,1,0:T(1,128)}), f32[8,1,256]{2,1,0:T(1,128)S(1)}, u32[]{:S(2)}, u32[]{:S(2)}) async-start(f32[8,1,256]{2,1,0:T(1,128)} %reshape.278), calls=%async_computation.2 | async-start | bytes 16384 | tf_op jit(solution)/shard_map/all_to_all | solution.py:127
  199.6 3.4 %copy-start.3 = (f32[512,4096]{1,0:T(8,128)S(1)}, f32[512,4096]{1,0:T(8,128)}, u32[]{:S(2)}) copy-start(f32[512,4096]{1,0:T(8,128)} %reshape.247) | copy-start | bytes 25165828
  212.2 23.9 %all-to-all-start = ((f32[8,8,4096]{2,1,0:T(8,128)}), f32[8,8,4096]{2,1,0:T(8,128)S(1)}, u32[]{:S(2)}, u32[]{:S(2)}) async-start(f32[8,8,4096]{2,1,0:T(8,128)} %fusion.4), calls=%async_computation | async-start | bytes 2097152 | tf_op jit(solution)/shard_map/all_to_all | solution.py:128
  236.6 41.0 %copy-start.1 = (bf16[8,32,4096]{2,1,0:T(8,128)(2,1)S(1)}, bf16[8,32,4096]{2,1,0:T(8,128)(2,1)}, u32[]{:S(2)}) copy-start(bf16[8,32,4096]{2,1,0:T(8,128)(2,1)} %param.20) | copy-start | bytes 6291460
where the time goes:
time: 279 us; the launch traced here: 278 us
  blocking collectives  150 us (54%)
  local copies, waits for them, and re-layouts  43.8 us (16%)
  matrix products  38.5 us (14%)
  starting transfers between devices  15.5 us (6%)
  waiting for transfers between devices  15.3 us (5%)
  other arithmetic  13.8 us (5%)
    psum x1, blocking collectives, shards(): lax.psum((query_part, key_part, value_part), 'mem')  74.8 us
    unnamed x1, blocking collectives  38.9 us
    all_gather x1, blocking collectives, shards(): lax.all_gather(attended, 'mem', axis=0, tiled=True)  31.3 us
    all_to_all x1, waiting for transfers between devices, shards(): lax.all_to_all(summed_flat, 'mem', split_axis=0, concat_axis=0, tiled=True)  15.3 us
    reshape x1, local copies, waits for them, and re-layouts, shards(): partial_value.reshape(pair_count, heads_local, HEAD_WIDTH)  9.39 us
    dot_general x1, matrix products, shards(): jnp.dot(pair_float, acc_scaled, precision=lax.Precision.HIGHEST)  9.16 us
    reduce_sum x1, other arithmetic, shards(): masses = jnp.sum(weights.astype(jnp.float32), axis=-1)  8.2 us
    transpose x1, local copies, waits for them, and re-layouts, shards(): jnp.einsum('phkgt,ptkd->phkgd', weights, page_values, preferred_element_t...  7.74 us
  transfers between devices with their start and end apart: 3, of which 1 were waited for; matrix products, arithmetic and copies ran while one was open for 18% of the time, Pallas kernels for 0%

commit v1 on v0

v1 whole, which is shorter than its diff:
```python
import functools
import math

import jax
import jax.numpy as jnp
from jax import lax
from jax.experimental import pallas as pl
from jax.experimental.pallas import tpu as pltpu
from jax.sharding import PartitionSpec as P

HEAD_WIDTH = 128
ADAPTER_RANK = 64
ADAPTER_COUNT = 32
MESH = pl.DeviceIdType.MESH
F32 = jnp.float32
BF16 = jnp.bfloat16
neg_floor = -1e30


def dot(x, y, dims=((1,), (0,))):
    return lax.dot_general(x, y, (dims, ((), ())), preferred_element_type=F32)


def kernel(
    n,
    group_size,
    hidden,
    adapter,
    slots,
    selection,
    wq,
    wk,
    wv,
    down,
    up,
    wo,
    kcache,
    vcache,
    out,
    dbuf,
    kvbuf,
    wqbuf,
    upbuf,
    kbuf,
    vbuf,
    wobuf,
    rtx,
    rrx,
    kvp,
    part,
    rx1,
    tx2,
    rx2,
    qfull,
    kvx,
    selx,
    acc,
    stat,
    resa,
    ress,
    rxa,
    rxs,
    txa,
    txs,
    fxa,
    fxs,
    cfull,
    outp,
    outr,
    loc,
    rsend,
    rrecv,
    s1,
    r1,
    s2,
    r2,
    ksem,
    gs,
    gr,
    hs,
    hr,
    as1,
    ar1,
    bs1,
    br1,
    as2,
    ar2,
    bs2,
    br2,
    osem,
):
    half = n // 2
    me = lax.axis_index("mem")
    core = lax.axis_index("tp")
    a = me // 2
    b = me % 2
    forks = hidden.shape[0]
    head_columns = wq.shape[1] // n
    per_owner = head_columns // HEAD_WIDTH
    wide = 2 * head_columns
    lanes = per_owner * forks
    both = 2 * lanes
    kv_local = wk.shape[1] // HEAD_WIDTH
    rank_local = up.shape[0]
    pages = kcache.shape[0]
    tokens = kcache.shape[1]
    sends = []

    def send(src, dst, ssem, rsem, where):
        copy = pltpu.make_async_remote_copy(
            src_ref=src,
            dst_ref=dst,
            send_sem=ssem,
            recv_sem=rsem,
            device_id=where,
            device_id_type=MESH,
        )
        copy.start()
        sends.append(copy)
        return copy

    def mate():
        return {"mem": me + 1 - 2 * b}

    def far(step):
        return {"mem": 2 * ((a + step) % half) + b}

    order = sorted(range(1, half), key=lambda d: -min(d, half - d)) + [0]
    locals_ = []

    def fetch(src, dst):
        copy = pltpu.make_async_copy(src, dst, loc.at[len(locals_)])
        copy.start()
        locals_.append(copy)
        return copy

    dchunks = dbuf.shape[0]
    dwide = dbuf.shape[2]
    get_down = [fetch(down.at[:, pl.ds(c * dwide, dwide)], dbuf.at[c]) for c in range(dchunks)]
    get_k = fetch(wk, kvbuf.at[0])
    get_v = fetch(wv, kvbuf.at[1])
    get_q, get_up = [], []
    for i, d in enumerate(order):
        columns = pl.ds(pl.multiple_of(((a + d) % half) * wide, wide), wide)
        get_q.append(fetch(wq.at[:, columns], wqbuf.at[i]))
        get_up.append(fetch(up.at[:, :, columns], upbuf.at[i]))
    get_kc = fetch(kcache, kbuf)
    get_vc = fetch(vcache, vbuf)
    get_wo = fetch(wo, wobuf)

    barrier = pltpu.get_barrier_semaphore()
    for o in range(1, n):
        pl.semaphore_signal(barrier, inc=1, device_id={"mem": (me + o) % n}, device_id_type=MESH)
    pl.semaphore_signal(barrier, inc=1, device_id={"tp": 1 - core}, device_id_type=MESH)

    h = hidden[...]
    ids = adapter[...].astype(F32)
    eye = lax.broadcasted_iota(jnp.int32, (forks, forks), 0) == lax.broadcasted_iota(
        jnp.int32, (forks, forks), 1
    )
    id_column = jnp.sum(jnp.where(eye, ids, 0.0), axis=1, keepdims=True)
    per_tile = 128 // ADAPTER_RANK
    lane_part = (
        lax.broadcasted_iota(jnp.int32, (forks, 128), 1) // ADAPTER_RANK
    ).astype(F32)
    folded = jnp.zeros((forks, 128), F32)
    for c in range(dchunks):
        get_down[c].wait()
        act = dot(h, dbuf[c])
        for t in range(dwide // 128):
            first = (c * (dwide // 128) + t) * per_tile
            folded += jnp.where(
                id_column - float(first) == lane_part, act[:, t * 128 : (t + 1) * 128], 0.0
            )
    turned = jnp.transpose(folded)
    rank_part = turned[:ADAPTER_RANK]
    for t in range(1, per_tile):
        rank_part += turned[t * ADAPTER_RANK : (t + 1) * ADAPTER_RANK]
    for j in range(n):
        rtx[j] = rank_part[j * rank_local : (j + 1) * rank_local]
    pl.semaphore_wait(barrier, n)
    rank_moves = []
    for o in range(1, n):
        to = (me + o) % n
        rank_moves.append(
            send(rtx.at[to], rrx.at[o], rsend.at[o], rrecv.at[o], {"mem": to})
        )

    get_k.wait()
    kp = dot(h, kvbuf[0])
    get_v.wait()
    vp = dot(h, kvbuf[1])
    for k in range(kv_local):
        kvp[0, k] = kp[:, k * HEAD_WIDTH : (k + 1) * HEAD_WIDTH]
        kvp[1, k] = vp[:, k * HEAD_WIDTH : (k + 1) * HEAD_WIDTH]

    slot_ids = me * pages + lax.broadcasted_iota(jnp.int32, (pages, slots.shape[1]), 0)
    match = (slots[...] == slot_ids).astype(F32).astype(BF16)
    chosen = dot(match, selection[...].astype(F32).astype(BF16), ((1,), (1,)))
    spread_eye = (
        lax.broadcasted_iota(jnp.int32, (forks, both), 1) % forks
        == lax.broadcasted_iota(jnp.int32, (forks, both), 0)
    ).astype(F32)
    spread_bf = spread_eye.astype(BF16)
    selx[...] = dot(chosen.astype(BF16), spread_bf)

    def kv_of(group):
        return (group * 2 * per_owner) // group_size

    get_q[0].wait()
    base = dot(h, wqbuf[0])
    for move in rank_moves:
        move.wait_recv()
    ranks = rtx[me]
    for o in range(1, n):
        ranks = ranks + rrx[o]
    ranks = ranks.astype(BF16).astype(F32)
    is_adapter = (
        lax.broadcasted_iota(jnp.int32, (ADAPTER_COUNT, forks), 0) == adapter[...]
    )
    rows = [
        jnp.where(is_adapter, ranks[r : r + 1], 0.0) for r in range(rank_local)
    ]
    spread = jnp.transpose(jnp.concatenate(rows, axis=0)).astype(BF16)

    moves1 = []
    for i, d in enumerate(order):
        if i:
            get_q[i].wait()
            base = dot(h, wqbuf[i])
        get_up[i].wait()
        total = base + dot(spread, upbuf[i].reshape(rank_local * ADAPTER_COUNT, wide))
        kv = kv_of((a + d) % half)
        for s in range(2):
            part[i, s, :, :head_columns] = total[:, s * head_columns : (s + 1) * head_columns]
            part[i, s, :, head_columns:] = kvp[s, kv]
        moves1.append(send(part.at[i, 1 - b], rx1.at[i], s1.at[i], r1.at[i], mate()))
    moves2 = []
    for i, d in enumerate(order):
        moves1[i].wait_recv()
        merged = part[i, b] + rx1[i]
        if d:
            tx2[i] = merged
            moves2.append(send(tx2.at[i], rx2.at[d], s2.at[d], r2.at[d], far(d)))
    for i, d in enumerate(order[:-1]):
        moves2[i].wait_recv()
        merged = merged + rx2[d]

    qfull[me] = merged[:, :head_columns].astype(BF16)
    kvx[b] = merged[:, head_columns:].astype(BF16)

    def gather(buf, ssem, rsem):
        near = send(buf.at[me], buf.at[me], ssem.at[0], rsem.at[0], mate())
        z = [
            send(buf.at[me], buf.at[me], ssem.at[d], rsem.at[d], far(d))
            for d in range(1, half)
        ]
        return near, z

    def forward(buf, ssem, rsem, z):
        passed = []
        for d in range(1, half):
            z[d - 1].wait_recv()
            slot = 2 * ((a + half - d) % half) + b
            passed.append(
                send(
                    buf.at[slot],
                    buf.at[slot],
                    ssem.at[half + d - 1],
                    rsem.at[half + d - 1],
                    mate(),
                )
            )
        return passed

    near, z = gather(qfull, gs, gr)
    kv_move = send(kvx.at[b], kvx.at[b], ksem.at[0], ksem.at[1], mate())

    scale = HEAD_WIDTH ** (-0.5)
    scale2 = scale * math.log2(math.e)

    def attend(j, group):
        kv = kv_of(group)
        columns = pl.ds(pl.multiple_of(kv * HEAD_WIDTH, HEAD_WIDTH), HEAD_WIDTH)
        pieces = []
        for s in range(2):
            for t in range(per_owner):
                pieces.append(qfull[2 * group + s, :, t * HEAD_WIDTH : (t + 1) * HEAD_WIDTH])
        queries = jnp.concatenate(pieces, axis=0)
        acc[...] = jnp.zeros_like(acc)
        top0 = jnp.full((1, both), neg_floor, F32)
        mass0 = jnp.zeros((1, both), F32)

        def page(p, carry):
            top, mass = carry
            keys = kbuf[p, :, columns]
            values = vbuf[p, :, columns]
            raw = dot(keys, queries, ((1,), (1,)))
            peak = jnp.max(raw, axis=0, keepdims=True)
            probs = jnp.exp2((raw - peak) * scale2).astype(BF16)
            page_mass = jnp.sum(probs.astype(F32), axis=0, keepdims=True)
            page_acc = dot(values, probs, ((0,), (0,)))
            hit = selx[pl.ds(p, 1), :] > 0.5
            peak = jnp.where(hit, peak, neg_floor)
            new_top = jnp.maximum(top, peak)
            fresh = jnp.where(hit, jnp.exp2((peak - new_top) * scale2), 0.0)
            keep = jnp.exp2((top - new_top) * scale2)
            acc[...] = acc[...] * keep + page_acc * fresh
            return new_top, mass * keep + page_mass * fresh

        top, mass = lax.fori_loop(0, pages, page, (top0, mass0), unroll=2)
        for s in range(2):
            part_lanes = slice(s * lanes, (s + 1) * lanes)
            resa[j, s] = acc[:, part_lanes].astype(BF16)
            ress[j, s, 0:1] = top[:, part_lanes]
            ress[j, s, 1:2] = mass[:, part_lanes]

    def join(items):
        top = items[0][1]
        for item in items[1:]:
            top = jnp.maximum(top, item[1])
        mass, total = 0.0, 0.0
        for x, t, w in items:
            factor = jnp.exp2((t - top) * scale2)
            mass = mass + w * factor
            total = total + x.astype(F32) * factor
        return total, top, mass

    moves3, moves4 = [], []

    def send_half(j):
        moves3.append(
            (
                send(resa.at[j, 1 - b], rxa.at[j], as1.at[j], ar1.at[j], mate()),
                send(ress.at[j, 1 - b], rxs.at[j], bs1.at[j], br1.at[j], mate()),
            )
        )

    def merge_half(j):
        for move in moves3[j]:
            move.wait_recv()
        total, top, mass = join(
            [
                (resa[j, b], ress[j, b, 0:1], ress[j, b, 1:2]),
                (rxa[j], rxs[j, 0:1], rxs[j, 1:2]),
            ]
        )
        if j == 0:
            return total, top, mass
        d = half - j
        txa[j] = total.astype(BF16)
        txs[j, 0:1] = top
        txs[j, 1:2] = mass
        moves4.append(
            (
                d,
                send(txa.at[j], fxa.at[d], as2.at[d], ar2.at[d], far(d)),
                send(txs.at[j], fxs.at[d], bs2.at[d], br2.at[d], far(d)),
            )
        )
        return None

    get_kc.wait()
    get_vc.wait()
    near.wait_recv()
    own_items = None
    passed = None
    for j in range(half):
        if j == 1:
            passed = forward(qfull, gs, gr, z)
        if j:
            passed[j - 1].wait_recv()
        attend(j, (a + half - j) % half)
        send_half(j)
        if j:
            result = merge_half(j - 1)
            if j == 1:
                own_items = result
    last = merge_half(half - 1)
    if half == 1:
        own_items = last

    kv_move.wait_recv()
    mine = jnp.concatenate(
        [qfull[me, :, t * HEAD_WIDTH : (t + 1) * HEAD_WIDTH] for t in range(per_owner)], axis=0
    )
    cross = dot(kvx[0], mine, ((1,), (1,)))
    own_eye = spread_eye[:, :lanes]
    own_score = jnp.sum(jnp.where(own_eye > 0.5, cross, 0.0), axis=0, keepdims=True)
    own_value = dot(kvx[1], own_eye.astype(BF16), ((0,), (0,)))
    items = [own_items, (own_value, own_score, jnp.ones((1, lanes), F32))]
    for d, move_a, move_s in moves4:
        move_a.wait_recv()
        move_s.wait_recv()
        items.append((fxa[d], fxs[d, 0:1], fxs[d, 1:2]))
    total, top, mass = join(items)
    context = jnp.transpose(total / mass)
    for t in range(per_owner):
        cfull[me, :, t * HEAD_WIDTH : (t + 1) * HEAD_WIDTH] = context[
            t * forks : (t + 1) * forks
        ].astype(BF16)

    near, z = gather(cfull, hs, hr)
    get_wo.wait()

    def project(slot):
        rows_ = pl.ds(pl.multiple_of(slot * head_columns, head_columns), head_columns)
        return dot(cfull[slot], wobuf[rows_, :])

    outp[...] = project(me)
    near.wait_recv()
    outp[...] += project(me + 1 - 2 * b)
    passed = forward(cfull, hs, hr, z)
    for d in range(1, half):
        outp[...] += project(2 * ((a + half - d) % half) + b)
    for d in range(1, half):
        passed[d - 1].wait_recv()
        outp[...] += project(2 * ((a + half - d) % half) + 1 - b)
    swap = send(outp, outr, osem.at[0], osem.at[1], {"tp": 1 - core})
    swap.wait_recv()
    out[...] = (outp[...] + outr[...]).astype(out.dtype)
    for copy in sends:
        copy.wait_send()


def shards(
    hidden,
    adapter,
    page_cache_slot,
    selection,
    query_projection_weight,
    key_projection_weight,
    value_projection_weight,
    adapter_down_weight,
    adapter_up_weight,
    output_projection_weight,
    prefix_key_cache,
    prefix_value_cache,
):
    n = lax.axis_size("mem")
    half = n // 2
    forks, depth = hidden.shape
    width = query_projection_weight.shape[1]
    kv_width = key_projection_weight.shape[1]
    kv_local = kv_width // HEAD_WIDTH
    group_size = width // kv_width
    columns = width // n
    lanes = (columns // HEAD_WIDTH) * forks
    out_width = output_projection_weight.shape[1]
    rank_local = adapter_up_weight.shape[0]
    pages, tokens = prefix_key_cache.shape[:2]
    down_width = adapter_down_weight.shape[1]
    chunks = 4
    dma = pltpu.SemaphoreType.DMA
    vmem = pltpu.VMEM
    scratch = [
        vmem((chunks, depth, down_width // chunks), BF16),
        vmem((2, depth, kv_width), BF16),
        vmem((half, depth, 2 * columns), BF16),
        vmem((half, rank_local, ADAPTER_COUNT, 2 * columns), BF16),
        vmem(prefix_key_cache.shape, BF16),
        vmem(prefix_value_cache.shape, BF16),
        vmem(output_projection_weight.shape, BF16),
        vmem((n, rank_local, forks), F32),
        vmem((n, rank_local, forks), F32),
        vmem((2, kv_local, forks, HEAD_WIDTH), F32),
        vmem((half, 2, forks, columns + HEAD_WIDTH), F32),
        vmem((half, forks, columns + HEAD_WIDTH), F32),
        vmem((half, forks, columns + HEAD_WIDTH), F32),
        vmem((half, forks, columns + HEAD_WIDTH), F32),
        vmem((n, forks, columns), BF16),
        vmem((2, forks, HEAD_WIDTH), BF16),
        vmem((pages, 2 * lanes), F32),
        vmem((HEAD_WIDTH, 2 * lanes), F32),
        vmem((8, 2 * lanes), F32),
        vmem((half, 2, HEAD_WIDTH, lanes), BF16),
        vmem((half, 2, 2, lanes), F32),
        vmem((half, HEAD_WIDTH, lanes), BF16),
        vmem((half, 2, lanes), F32),
        vmem((half, HEAD_WIDTH, lanes), BF16),
        vmem((half, 2, lanes), F32),
        vmem((half, HEAD_WIDTH, lanes), BF16),
        vmem((half, 2, lanes), F32),
        vmem((n, forks, columns), BF16),
        vmem((forks, out_width), F32),
        vmem((forks, out_width), F32),
        dma((chunks + 2 + 2 * half + 3,)),
        dma((n,)),
        dma((n,)),
        dma((half,)),
        dma((half,)),
        dma((half,)),
        dma((half,)),
        dma((2,)),
        dma((n,)),
        dma((n,)),
        dma((n,)),
        dma((n,)),
        dma((half,)),
        dma((half,)),
        dma((half,)),
        dma((half,)),
        dma((half,)),
        dma((half,)),
        dma((half,)),
        dma((half,)),
        dma((2,)),
    ]
    small = pl.BlockSpec(memory_space=pltpu.VMEM)
    large = pl.BlockSpec(memory_space=pl.ANY)
    return pl.pallas_call(
        functools.partial(kernel, n, group_size),
        out_shape=jax.ShapeDtypeStruct((forks, out_width), BF16),
        in_specs=[small] * 4 + [large] * 8,
        out_specs=small,
        scratch_shapes=scratch,
        compiler_params=pltpu.CompilerParams(
            collective_id=0, has_side_effects=True, vmem_limit_bytes=60 * 1024 * 1024
        ),
    )(
        hidden,
        adapter.reshape(1, forks),
        page_cache_slot.reshape(1, page_cache_slot.shape[0]),
        selection,
        query_projection_weight,
        key_projection_weight,
        value_projection_weight,
        adapter_down_weight,
        adapter_up_weight,
        output_projection_weight,
        prefix_key_cache,
        prefix_value_cache,
    )


def solution(mesh):
    return jax.shard_map(
        shards,
        mesh=mesh,
        in_specs=(
            P("groups", "mem"),
            P("groups"),
            P("groups"),
            P("groups", None),
            P("mem", "tp"),
            P("mem", "tp"),
            P("mem", "tp"),
            P("mem", None),
            P("mem", None, "tp"),
            P("tp", "mem"),
            P(("groups", "mem"), None, "tp"),
            P(("groups", "mem"), None, "tp"),
        ),
        out_specs=P("groups", "mem"),
        check_vma=False,
    )
```

time: 279 us -> 82 us (0.29)
  blocking collectives: 150 us -> 0 us
  Pallas kernels: 0 us -> 80.3 us
  local copies, waits for them, and re-layouts: 43.8 us -> 1.57 us
  matrix products: 38.5 us -> 0 us
  starting transfers between devices: 15.5 us -> 0 us
  waiting for transfers between devices: 15.3 us -> 0 us
  other arithmetic: 13.8 us -> 0 us
    pallas_call x0 -> x1, Pallas kernels: none -> 80.3 us  [shards(): pl.pallas_call(functools.partial(kernel, n, group_size), out_shape=jax.Sh...]
    psum x2 -> x0, blocking collectives: 79.4 us -> none  [the longest x1 74.8 us: shards(): lax.psum((query_part, key_part, value_part), 'mem')]
    unnamed x1 -> x0, blocking collectives: 38.9 us -> none
    dot_general x10 -> x0, matrix products: 38.3 us -> none  [the longest x1 9.16 us: shards(): jnp.dot(pair_float, acc_scaled, precision=lax.Precision.HIGHEST)]
    all_gather x1 -> x0, blocking collectives: 31.3 us -> none  [shards(): lax.all_gather(attended, 'mem', axis=0, tiled=True)]
    reshape x6 -> x0, local copies, waits for them, and re-layouts: 19.1 us -> none  [the longest x1 9.39 us: shards(): partial_value.reshape(pair_count, heads_local, HEAD_WIDTH)]
    all_to_all x3 -> x0, starting transfers between devices: 15.5 us -> none  [the longest x1 6 us: shards(): lax.all_to_all(summed_flat, 'mem', split_axis=0, concat_axis=0, tiled=True)]
    all_to_all x3 -> x0, waiting for transfers between devices: 15.3 us -> none  [the longest x1 15.3 us: shards(): lax.all_to_all(summed_flat, 'mem', split_axis=0, concat_axis=0, tiled=True)]
  transfers between devices with their start and end apart: 3 -> 0, of which waited for: 1 -> 0; matrix products, arithmetic and copies ran while one was open for 18% -> 0% of each run, Pallas kernels for 0% -> 0%
where the time goes in v1:
time: 82 us; the launch traced here: 81.9 us
  Pallas kernels  80.3 us (98%)
  local copies, waits for them, and re-layouts  1.57 us (2%)
    pallas_call x1, Pallas kernels, shards(): pl.pallas_call(functools.partial(kernel, n, group_size), out_shape=jax.Sh...  80.3 us

profile of v1, /device:TPU:0, one launch (start us, length us, event | category | flops | bytes accessed | tf_op | source)
XLA Modules:
  0.0 81.9 jit_solution(16972899423927673936)
XLA Ops:
  0.0 80.3 %shard_map.118 = bf16[64,1024]{1,0:T(8,128)(2,1)} custom-call(bf16[64,1024]{1,0:T(8,128)(2,1)} %hidden.1, s32[1,64]{1,0:T(1,128)} %bitcast.2, s32[1,128]{1,0:T(1,128)} %bitcast.3, s32[64,128]{1,0:T(8,128)} %selection.1, bf16[1024,4096]{1,0:T(8,128)(2,1)} %wq.1, bf16[1024,512]{1,0:T(8,128)(2,1)} %wk.1, bf16[1024,512]{1,0:T(8,128)(2,1)} %wv.1, ...), custom_call_target="tpu_custom_call" | custom-call | tf_op jit(solution)/shard_map/pallas_call | solution.py:511
  80.3 1.6 %copy.14 = bf16[64,1024]{1,0:T(8,128)(2,1)} copy(bf16[64,1024]{1,0:T(8,128)(2,1)} %shard_map.118) | data formatting | bytes 262144

commit v2 on v1

--- a/solution.py
+++ b/solution.py
@@ -43,10 +43,13 @@
     upbuf,
     kbuf,
     vbuf,
+    vtbuf,
     wobuf,
     rtx,
     rrx,
     kvp,
+    kpart,
+    krx,
     part,
     rx1,
     tx2,
@@ -55,7 +58,6 @@
     kvx,
     selx,
     acc,
-    stat,
     resa,
     ress,
     rxa,
@@ -140,13 +142,13 @@
     get_k = fetch(wk, kvbuf.at[0])
     get_v = fetch(wv, kvbuf.at[1])
     get_q, get_up = [], []
-    for i, d in enumerate(order):
-        columns = pl.ds(pl.multiple_of(((a + d) % half) * wide, wide), wide)
+
+    def fetch_piece(i):
+        columns = pl.ds(pl.multiple_of(((a + order[i]) % half) * wide, wide), wide)
         get_q.append(fetch(wq.at[:, columns], wqbuf.at[i]))
         get_up.append(fetch(up.at[:, :, columns], upbuf.at[i]))
-    get_kc = fetch(kcache, kbuf)
-    get_vc = fetch(vcache, vbuf)
-    get_wo = fetch(wo, wobuf)
+
+    fetch_piece(0)
 
     barrier = pltpu.get_barrier_semaphore()
     for o in range(1, n):
@@ -172,6 +174,8 @@
             folded += jnp.where(
                 id_column - float(first) == lane_part, act[:, t * 128 : (t + 1) * 128], 0.0
             )
+    for i in range(1, half):
+        fetch_piece(i)
     turned = jnp.transpose(folded)
     rank_part = turned[:ADAPTER_RANK]
     for t in range(1, per_tile):
@@ -186,13 +190,22 @@
             send(rtx.at[to], rrx.at[o], rsend.at[o], rrecv.at[o], {"mem": to})
         )
 
+    def kv_of(group):
+        return (group * 2 * per_owner) // group_size
+
     get_k.wait()
     kp = dot(h, kvbuf[0])
     get_v.wait()
     vp = dot(h, kvbuf[1])
+    get_vc = fetch(vcache, vbuf)
+    get_kc = fetch(kcache, kbuf)
     for k in range(kv_local):
         kvp[0, k] = kp[:, k * HEAD_WIDTH : (k + 1) * HEAD_WIDTH]
         kvp[1, k] = vp[:, k * HEAD_WIDTH : (k + 1) * HEAD_WIDTH]
+    for i, d in enumerate(order):
+        for s in range(2):
+            kpart[s, i] = kvp[s, kv_of((a + d) % half)]
+    move_kv = send(kpart.at[1 - b], krx, ksem.at[2], ksem.at[3], mate())
 
     slot_ids = me * pages + lax.broadcasted_iota(jnp.int32, (pages, slots.shape[1]), 0)
     match = (slots[...] == slot_ids).astype(F32).astype(BF16)
@@ -203,9 +216,6 @@
     ).astype(F32)
     spread_bf = spread_eye.astype(BF16)
     selx[...] = dot(chosen.astype(BF16), spread_bf)
-
-    def kv_of(group):
-        return (group * 2 * per_owner) // group_size
 
     get_q[0].wait()
     base = dot(h, wqbuf[0])
@@ -230,18 +240,32 @@
             base = dot(h, wqbuf[i])
         get_up[i].wait()
         total = base + dot(spread, upbuf[i].reshape(rank_local * ADAPTER_COUNT, wide))
-        kv = kv_of((a + d) % half)
         for s in range(2):
-            part[i, s, :, :head_columns] = total[:, s * head_columns : (s + 1) * head_columns]
-            part[i, s, :, head_columns:] = kvp[s, kv]
+            part[i, s] = total[:, s * head_columns : (s + 1) * head_columns]
         moves1.append(send(part.at[i, 1 - b], rx1.at[i], s1.at[i], r1.at[i], mate()))
+    get_wo = fetch(wo, wobuf)
     moves2 = []
+    get_vc.wait()
+    vtbuf[:, :, HEAD_WIDTH:, :] = jnp.ones(
+        (pages, kv_local, vtbuf.shape[2] - HEAD_WIDTH, tokens), BF16
+    )
+
+    def turn(p, carry):
+        for k in range(kv_local):
+            block = vbuf[p, :, k * HEAD_WIDTH : (k + 1) * HEAD_WIDTH]
+            vtbuf[p, k, :HEAD_WIDTH, :] = jnp.transpose(block)
+        return carry
+
     for i, d in enumerate(order):
+        lax.fori_loop(pages * i // half, pages * (i + 1) // half, turn, 0)
+        if i == 0:
+            move_kv.wait_recv()
         moves1[i].wait_recv()
-        merged = part[i, b] + rx1[i]
+        tx2[i, :, :head_columns] = part[i, b] + rx1[i]
+        tx2[i, :, head_columns:] = kpart[b, i] + krx[i]
         if d:
-            tx2[i] = merged
             moves2.append(send(tx2.at[i], rx2.at[d], s2.at[d], r2.at[d], far(d)))
+    merged = tx2[half - 1]
     for i, d in enumerate(order[:-1]):
         moves2[i].wait_recv()
         merged = merged + rx2[d]
@@ -276,6 +300,7 @@
     near, z = gather(qfull, gs, gr)
     kv_move = send(kvx.at[b], kvx.at[b], ksem.at[0], ksem.at[1], mate())
 
+    batch = math.gcd(pages, 4)
     scale = HEAD_WIDTH ** (-0.5)
     scale2 = scale * math.log2(math.e)
 
@@ -291,24 +316,33 @@
         top0 = jnp.full((1, both), neg_floor, F32)
         mass0 = jnp.zeros((1, both), F32)
 
-        def page(p, carry):
+        def block(q, carry):
             top, mass = carry
-            keys = kbuf[p, :, columns]
-            values = vbuf[p, :, columns]
-            raw = dot(keys, queries, ((1,), (1,)))
-            peak = jnp.max(raw, axis=0, keepdims=True)
-            probs = jnp.exp2((raw - peak) * scale2).astype(BF16)
-            page_mass = jnp.sum(probs.astype(F32), axis=0, keepdims=True)
-            page_acc = dot(values, probs, ((0,), (0,)))
-            hit = selx[pl.ds(p, 1), :] > 0.5
-            peak = jnp.where(hit, peak, neg_floor)
-            new_top = jnp.maximum(top, peak)
-            fresh = jnp.where(hit, jnp.exp2((peak - new_top) * scale2), 0.0)
+            first = q * batch
+            keys = kbuf[pl.ds(first, batch), :, columns].reshape(batch * tokens, HEAD_WIDTH)
+            raw_all = dot(keys, queries, ((1,), (1,)))
+            found = []
+            new_top = top
+            for u in range(batch):
+                raw = raw_all[u * tokens : (u + 1) * tokens]
+                peak = jnp.max(raw, axis=0, keepdims=True)
+                probs = jnp.exp2((raw - peak) * scale2).astype(BF16)
+                sums = dot(vtbuf[first + u, kv], probs)
+                hit = selx[pl.ds(first + u, 1), :] > 0.5
+                peak = jnp.where(hit, peak, neg_floor)
+                new_top = jnp.maximum(new_top, peak)
+                found.append((hit, peak, sums))
             keep = jnp.exp2((top - new_top) * scale2)
-            acc[...] = acc[...] * keep + page_acc * fresh
-            return new_top, mass * keep + page_mass * fresh
-
-        top, mass = lax.fori_loop(0, pages, page, (top0, mass0), unroll=2)
+            mass = mass * keep
+            total = acc[...] * keep
+            for hit, peak, sums in found:
+                fresh = jnp.where(hit, jnp.exp2((peak - new_top) * scale2), 0.0)
+                total = total + sums[:HEAD_WIDTH] * fresh
+                mass = mass + sums[HEAD_WIDTH : HEAD_WIDTH + 1] * fresh
+            acc[...] = total
+            return new_top, mass
+
+        top, mass = lax.fori_loop(0, pages // batch, block, (top0, mass0))
         for s in range(2):
             part_lanes = slice(s * lanes, (s + 1) * lanes)
             resa[j, s] = acc[:, part_lanes].astype(BF16)
@@ -361,7 +395,6 @@
         return None
 
     get_kc.wait()
-    get_vc.wait()
     near.wait_recv()
     own_items = None
     passed = None
@@ -460,19 +493,21 @@
         vmem((half, rank_local, ADAPTER_COUNT, 2 * columns), BF16),
         vmem(prefix_key_cache.shape, BF16),
         vmem(prefix_value_cache.shape, BF16),
+        vmem((pages, kv_local, HEAD_WIDTH + 16, tokens), BF16),
         vmem(output_projection_weight.shape, BF16),
         vmem((n, rank_local, forks), F32),
         vmem((n, rank_local, forks), F32),
         vmem((2, kv_local, forks, HEAD_WIDTH), F32),
-        vmem((half, 2, forks, columns + HEAD_WIDTH), F32),
-        vmem((half, forks, columns + HEAD_WIDTH), F32),
+        vmem((2, half, forks, HEAD_WIDTH), F32),
+        vmem((half, forks, HEAD_WIDTH), F32),
+        vmem((half, 2, forks, columns), F32),
+        vmem((half, forks, columns), F32),
         vmem((half, forks, columns + HEAD_WIDTH), F32),
         vmem((half, forks, columns + HEAD_WIDTH), F32),
         vmem((n, forks, columns), BF16),
         vmem((2, forks, HEAD_WIDTH), BF16),
         vmem((pages, 2 * lanes), F32),
         vmem((HEAD_WIDTH, 2 * lanes), F32),
-        vmem((8, 2 * lanes), F32),
         vmem((half, 2, HEAD_WIDTH, lanes), BF16),
         vmem((half, 2, 2, lanes), F32),
         vmem((half, HEAD_WIDTH, lanes), BF16),
@@ -491,7 +526,7 @@
         dma((half,)),
         dma((half,)),
         dma((half,)),
-        dma((2,)),
+        dma((4,)),
         dma((n,)),
         dma((n,)),
         dma((n,)),

time: 82 us -> 71.7 us (0.87)
  Pallas kernels: 80.3 us -> 70 us
    pallas_call x1, Pallas kernels: 80.3 us -> 70 us  [shards(): pl.pallas_call(functools.partial(kernel, n, group_size), out_shape=jax.Sh...]
where the time goes in v2:
time: 71.7 us; the launch traced here: 71.6 us
  Pallas kernels  70 us (98%)
  local copies, waits for them, and re-layouts  1.57 us (2%)
    pallas_call x1, Pallas kernels, shards(): pl.pallas_call(functools.partial(kernel, n, group_size), out_shape=jax.Sh...  70 us
    unnamed x1, local copies, waits for them, and re-layouts  1.57 us

profile of v2, /device:TPU:0, one launch (start us, length us, event | category | flops | bytes accessed | tf_op | source)
XLA Modules:
  0.0 71.6 jit_solution(13011484477784706760)
XLA Ops:
  0.0 70.0 %shard_map.118 = bf16[64,1024]{1,0:T(8,128)(2,1)} custom-call(bf16[64,1024]{1,0:T(8,128)(2,1)} %hidden.1, s32[1,64]{1,0:T(1,128)} %bitcast.2, s32[1,128]{1,0:T(1,128)} %bitcast.3, s32[64,128]{1,0:T(8,128)} %selection.1, bf16[1024,4096]{1,0:T(8,128)(2,1)} %wq.1, bf16[1024,512]{1,0:T(8,128)(2,1)} %wk.1, bf16[1024,512]{1,0:T(8,128)(2,1)} %wv.1, ...), custom_call_target="tpu_custom_call" | custom-call | tf_op jit(solution)/shard_map/pallas_call | solution.py:546
  70.0 1.6 %copy.14 = bf16[64,1024]{1,0:T(8,128)(2,1)} copy(bf16[64,1024]{1,0:T(8,128)(2,1)} %shard_map.118) | data formatting | bytes 262144

commit v3 on v2

--- a/solution.py
+++ b/solution.py
@@ -15,6 +15,8 @@
 F32 = jnp.float32
 BF16 = jnp.bfloat16
 neg_floor = -1e30
+UNROLL = 1
+BATCH = 8
 
 
 def dot(x, y, dims=((1,), (0,))):
@@ -50,6 +52,8 @@
     kvp,
     kpart,
     krx,
+    tk2,
+    rk2,
     part,
     rx1,
     tx2,
@@ -77,6 +81,8 @@
     s2,
     r2,
     ksem,
+    ks2,
+    kr2,
     gs,
     gr,
     hs,
@@ -243,6 +249,15 @@
         for s in range(2):
             part[i, s] = total[:, s * head_columns : (s + 1) * head_columns]
         moves1.append(send(part.at[i, 1 - b], rx1.at[i], s1.at[i], r1.at[i], mate()))
+        if i == 0:
+            move_kv.wait_recv()
+            moves_kv = []
+            for e, step in enumerate(order):
+                tk2[e] = kpart[b, e] + krx[e]
+                if step:
+                    moves_kv.append(
+                        send(tk2.at[e], rk2.at[step], ks2.at[step], kr2.at[step], far(step))
+                    )
     get_wo = fetch(wo, wobuf)
     moves2 = []
     get_vc.wait()
@@ -258,20 +273,21 @@
 
     for i, d in enumerate(order):
         lax.fori_loop(pages * i // half, pages * (i + 1) // half, turn, 0)
-        if i == 0:
-            move_kv.wait_recv()
         moves1[i].wait_recv()
-        tx2[i, :, :head_columns] = part[i, b] + rx1[i]
-        tx2[i, :, head_columns:] = kpart[b, i] + krx[i]
+        tx2[i] = part[i, b] + rx1[i]
         if d:
             moves2.append(send(tx2.at[i], rx2.at[d], s2.at[d], r2.at[d], far(d)))
     merged = tx2[half - 1]
     for i, d in enumerate(order[:-1]):
         moves2[i].wait_recv()
         merged = merged + rx2[d]
-
-    qfull[me] = merged[:, :head_columns].astype(BF16)
-    kvx[b] = merged[:, head_columns:].astype(BF16)
+    merged_kv = tk2[half - 1]
+    for i, d in enumerate(order[:-1]):
+        moves_kv[i].wait_recv()
+        merged_kv = merged_kv + rk2[d]
+
+    qfull[me] = merged.astype(BF16)
+    kvx[b] = merged_kv.astype(BF16)
 
     def gather(buf, ssem, rsem):
         near = send(buf.at[me], buf.at[me], ssem.at[0], rsem.at[0], mate())
@@ -281,9 +297,9 @@
         ]
         return near, z
 
-    def forward(buf, ssem, rsem, z):
+    def forward(buf, ssem, rsem, z, steps):
         passed = []
-        for d in range(1, half):
+        for d in steps:
             z[d - 1].wait_recv()
             slot = 2 * ((a + half - d) % half) + b
             passed.append(
@@ -300,7 +316,7 @@
     near, z = gather(qfull, gs, gr)
     kv_move = send(kvx.at[b], kvx.at[b], ksem.at[0], ksem.at[1], mate())
 
-    batch = math.gcd(pages, 4)
+    batch = math.gcd(pages, BATCH)
     scale = HEAD_WIDTH ** (-0.5)
     scale2 = scale * math.log2(math.e)
 
@@ -342,7 +358,11 @@
             acc[...] = total
             return new_top, mass
 
-        top, mass = lax.fori_loop(0, pages // batch, block, (top0, mass0))
+        blocks = pages // batch
+        state = lax.fori_loop(0, blocks // 2, block, (top0, mass0), unroll=UNROLL)
+        if j == 0 and half > 1:
+            passed.extend(forward(qfull, gs, gr, z, [1]))
+        top, mass = lax.fori_loop(blocks // 2, blocks, block, state, unroll=UNROLL)
         for s in range(2):
             part_lanes = slice(s * lanes, (s + 1) * lanes)
             resa[j, s] = acc[:, part_lanes].astype(BF16)
@@ -397,10 +417,10 @@
     get_kc.wait()
     near.wait_recv()
     own_items = None
-    passed = None
+    passed = []
     for j in range(half):
         if j == 1:
-            passed = forward(qfull, gs, gr, z)
+            passed += forward(qfull, gs, gr, z, range(2, half))
         if j:
             passed[j - 1].wait_recv()
         attend(j, (a + half - j) % half)
@@ -443,7 +463,7 @@
     outp[...] = project(me)
     near.wait_recv()
     outp[...] += project(me + 1 - 2 * b)
-    passed = forward(cfull, hs, hr, z)
+    passed = forward(cfull, hs, hr, z, range(1, half))
     for d in range(1, half):
         outp[...] += project(2 * ((a + half - d) % half) + b)
     for d in range(1, half):
@@ -500,10 +520,12 @@
         vmem((2, kv_local, forks, HEAD_WIDTH), F32),
         vmem((2, half, forks, HEAD_WIDTH), F32),
         vmem((half, forks, HEAD_WIDTH), F32),
+        vmem((half, forks, HEAD_WIDTH), F32),
+        vmem((half, forks, HEAD_WIDTH), F32),
         vmem((half, 2, forks, columns), F32),
         vmem((half, forks, columns), F32),
-        vmem((half, forks, columns + HEAD_WIDTH), F32),
-        vmem((half, forks, columns + HEAD_WIDTH), F32),
+        vmem((half, forks, columns), F32),
+        vmem((half, forks, columns), F32),
         vmem((n, forks, columns), BF16),
         vmem((2, forks, HEAD_WIDTH), BF16),
         vmem((pages, 2 * lanes), F32),
@@ -527,6 +549,8 @@
         dma((half,)),
         dma((half,)),
         dma((4,)),
+        dma((half,)),
+        dma((half,)),
         dma((n,)),
         dma((n,)),
         dma((n,)),

time: 71.7 us -> 65.4 us (0.912)
  Pallas kernels: 70 us -> 63.6 us
    pallas_call x1, Pallas kernels: 70 us -> 63.6 us  [shards(): pl.pallas_call(functools.partial(kernel, n, group_size), out_shape=jax.Sh...]
where the time goes in v3:
time: 65.4 us; the launch traced here: 65.2 us
  Pallas kernels  63.6 us (97%)
  local copies, waits for them, and re-layouts  1.57 us (2%)
    pallas_call x1, Pallas kernels, shards(): pl.pallas_call(functools.partial(kernel, n, group_size), out_shape=jax.Sh...  63.6 us
    unnamed x1, local copies, waits for them, and re-layouts  1.57 us

profile of v3, /device:TPU:0, one launch (start us, length us, event | category | flops | bytes accessed | tf_op | source)
XLA Modules:
  0.0 65.2 jit_solution(81098747792951418)
XLA Ops:
  0.0 63.6 %shard_map.118 = bf16[64,1024]{1,0:T(8,128)(2,1)} custom-call(bf16[64,1024]{1,0:T(8,128)(2,1)} %hidden.1, s32[1,64]{1,0:T(1,128)} %bitcast.2, s32[1,128]{1,0:T(1,128)} %bitcast.3, s32[64,128]{1,0:T(8,128)} %selection.1, bf16[1024,4096]{1,0:T(8,128)(2,1)} %wq.1, bf16[1024,512]{1,0:T(8,128)(2,1)} %wk.1, bf16[1024,512]{1,0:T(8,128)(2,1)} %wv.1, ...), custom_call_target="tpu_custom_call" | custom-call | tf_op jit(solution)/shard_map/pallas_call | solution.py:570
  63.6 1.6 %copy.14 = bf16[64,1024]{1,0:T(8,128)(2,1)} copy(bf16[64,1024]{1,0:T(8,128)(2,1)} %shard_map.118) | data formatting | bytes 262144
